TPU v7x, 32 devices: a whole 2x2x4 slice. The times are simulated.
32 devices in a mesh: samp: 8 (over y, x, core), blk: 4 (over z).
Axes of the slice: x: 2, y: 2, z: 4, core: 2. Of those that a mesh axis runs over, the one named last changes fastest.
Arguments:
- genotypes: int32 [16384, 6144], P('samp', 'blk'), may hold values from 0 to 2
- phenotype: float32 [16384], P('samp'), may hold values from -15 to 15
- fold_ids: int32 [16384], P('samp'), may hold values from 0 to 4, as said below
Outputs:
- coeff_all: float32 [6144, 400], P('blk')
- fold_scores: float32 [2, 400], replicated
Inputs may be any that keep to these rules, and one draw needn't show every extreme that they name: `fold_ids`: every fold holds 3276 or 3277 people.
All inputs are finite; a program needn't handle non-finite values.
Results may differ from a plain program's by a relative error of at most 0.0003.
Values sent between devices are 32-bit elements; how exact they have to be, the bound alone decides.
A program may use at most 128 MiB of HBM per device.

v0:
```python
import math

import jax
import jax.numpy as jnp
from jax import lax
from jax.sharding import PartitionSpec as P

FOLDS = 5
LAMBDAS = 20
SWEEPS = 3
GRID = 400


step_size = 0.6
epsilon = 1e-05
lambda_base = 0.1
lambda_ratio = 1.2
shrink_unit = 0.2
highest = lax.Precision.HIGHEST


def grid_tables():
    column = jnp.arange(GRID)
    fold_of = column % FOLDS
    levels = column // FOLDS % LAMBDAS
    penalty = lambda_base * jnp.exp(levels.astype(jnp.float32) * math.log(lambda_ratio))
    shrink = shrink_unit * (column // (FOLDS * LAMBDAS) + 1).astype(jnp.float32)
    return (fold_of, penalty, shrink)


def soft_threshold(values, cutoff):
    return values - jnp.clip(values, -cutoff, cutoff)


def local(genotypes, phenotype, fold_ids):
    num_rows, block_width = genotypes.shape
    sample_count = num_rows * lax.axis_size("samp")
    snp_total = block_width * lax.axis_size("blk")
    dosage_bf = genotypes.astype(jnp.bfloat16)
    onehot = fold_ids[:, None] == jnp.arange(FOLDS)[None, :]
    pheno_split = jnp.where(onehot, phenotype[:, None], 0.0)
    local_sum = jnp.sum(genotypes, axis=0).astype(jnp.float32)
    local_sq = jnp.sum(genotypes * genotypes, axis=0).astype(jnp.float32)
    local_geno_pheno = jnp.dot(pheno_split.T, genotypes.astype(jnp.float32), precision=highest)
    local_pheno_sum = jnp.sum(pheno_split, axis=0)
    local_count = jnp.sum(onehot.astype(jnp.int32), axis=0).astype(jnp.float32)
    fold_of, penalty, shrink = grid_tables()
    column_fold = fold_of[None, :] == jnp.arange(FOLDS)[:, None]
    gram_local = jnp.dot(dosage_bf.T, dosage_bf, preferred_element_type=jnp.float32)
    gram_sum, geno_sum, geno_sq, geno_pheno, fold_pheno_sum, fold_count = lax.psum(
        (gram_local, local_sum, local_sq, local_geno_pheno, local_pheno_sum, local_count), "samp"
    )
    snp_mean = geno_sum / sample_count
    scales = jnp.sqrt(geno_sq / sample_count - snp_mean * snp_mean + epsilon)
    train_geno = jnp.sum(geno_pheno, axis=0)[None, :] - geno_pheno
    train_pheno = jnp.sum(fold_pheno_sum) - fold_pheno_sum
    zscore = (train_geno - train_pheno[:, None] * snp_mean[None, :]) / (
        scales[None, :] * jnp.sqrt(sample_count - fold_count)[:, None]
    )
    snp_mean, scales, zscore = (snp_mean, scales, zscore)
    ld_block = (gram_sum / sample_count - snp_mean[:, None] * snp_mean[None, :]) / (
        scales[:, None] * scales[None, :]
    )
    col_share = GRID // lax.axis_size("samp")
    first_col = lax.axis_index("samp") * col_share
    target = lax.dynamic_slice_in_dim(
        jnp.sum(jnp.where(column_fold[None, :, :], zscore.T[:, :, None], 0.0), axis=1),
        first_col,
        col_share,
        1,
    )
    penalty_mine = lax.dynamic_slice_in_dim(penalty, first_col, col_share, 0)
    shrink_mine = lax.dynamic_slice_in_dim(shrink, first_col, col_share, 0)
    coeffs = soft_threshold(step_size * target, step_size * penalty_mine)
    for sweep_idx in range(SWEEPS - 1):
        gradient = (
            (1.0 - shrink_mine) * jnp.dot(ld_block, coeffs, precision=highest)
            + shrink_mine * coeffs
            - target
        )
        coeffs = soft_threshold(coeffs - step_size * gradient, step_size * penalty_mine)
    coeff_all = lax.all_gather(coeffs, "samp", axis=1, tiled=True)
    weighted = (coeff_all / scales[:, None]).astype(jnp.bfloat16)
    offset = jnp.dot(snp_mean[None, :], weighted.astype(jnp.float32), precision=highest)
    partial_value = jnp.dot(dosage_bf, weighted, preferred_element_type=jnp.float32) - offset
    root_snps = math.sqrt(snp_total)
    col_part = GRID // lax.axis_size("blk")
    part_first = lax.axis_index("blk") * col_part
    predicted = lax.psum_scatter(partial_value, "blk", scatter_dimension=1, tiled=True) / root_snps
    fold_slice = lax.dynamic_slice_in_dim(fold_of, part_first, col_part, 0)
    chosen = fold_ids[:, None] == fold_slice[None, :]
    numerator = jnp.sum(jnp.where(chosen, predicted * phenotype[:, None], 0.0), axis=0)
    denominator = jnp.sum(jnp.where(chosen, predicted * predicted, 0.0), axis=0)
    numerator, denominator = lax.psum((numerator, denominator), "samp")
    slice_fold = fold_slice[None, :] == jnp.arange(FOLDS)[:, None]
    counts = jnp.sum(jnp.where(slice_fold, fold_count[:, None], 0.0), axis=0)
    piece_scores = jnp.stack([numerator / counts, denominator / counts])
    fold_scores = lax.all_gather(piece_scores, "blk", axis=1, tiled=True)
    return (coeff_all, fold_scores)


def solution(mesh):
    return jax.shard_map(
        local,
        mesh=mesh,
        in_specs=(P("samp", "blk"), P("samp"), P("samp")),
        out_specs=(P("blk", None), P()),
        check_vma=False,
    )
```

profile of v0, /device:TPU:0, one launch (start us, length us, event | category | flops | bytes accessed | tf_op | source)
XLA Modules:
  0.0 336.0 jit_solution(6285634921455484251)
XLA Ops:
  7.2 19.0 %fusion.5 = f32[1536,1536]{1,0:T(8,128)} fusion(s32[2048,1536]{1,0:T(8,128)} %param.3), kind=kOutput, calls=%fused_computation.8 | convolution fusion | flops 9666822144 | bytes 22020096 | tf_op jit(solution)/shard_map/dot_general | solution.py:49
  26.2 0.2 all-gather.4.cloned.1.call-start
  26.5 6.1 %fusion.53 = (s32[1536]{0:T(1024)S(1)}, s32[1536]{0:T(1024)S(1)}) fusion(s32[2048,1536]{1,0:T(8,128)} %param.3), kind=kLoop, calls=%fused_computation.86 | loop fusion | flops 9434112 | bytes 12595200 | tf_op jit(solution)/shard_map/reduce_sum | solution.py:42
  32.6 0.1 convert_reduce_fusion
  32.7 0.1 select_reduce_fusion.1
  32.8 1.9 copy-done
  34.7 6.2 %fusion.1 = f32[5,1536]{1,0:T(8,128)S(1)} fusion(s32[2048,1536]{1,0:T(8,128)S(1)} %copy-done, f32[2048]{0:T(1024)S(1)} %copy-done.3, s32[2048]{0:T(1024)S(1)} %copy-done.2), kind=kOutput, calls=%fused_computation.1 | convolution fusion | flops 191909888 | bytes 12630016 | tf_op jit(solution)/shard_map/dot_general | solution.py:44
  41.0 30.4 %all-reduce.3 = (f32[1536]{0:T(1024)S(1)}, f32[1536]{0:T(1024)S(1)}, f32[5,1536]{1,0:T(8,128)S(1)}, f32[5]{0:T(128)S(1)}, f32[5]{0:T(128)S(1)}) all-reduce(f32[1536]{0:T(1024)S(1)} %convert_element_type.30, f32[1536]{0:T(1024)S(1)} %convert_element_type.29, f32[5,1536]{1,0:T(8,128)S(1)} %fusion.1, ...), channel_id=1, replica_groups=mesh['samp'=8,'blk'=4] {'samp'}, use_global_device_ids=true, to_apply=%region_8.9 | all-reduce | flops 10762 | bytes 86096 | tf_op jit(solution)/shard_map/psum | solution.py:50
  71.3 0.6 reduce_sum.92
  72.0 0.1 broadcast_subtract_fusion
  72.1 0.7 subtract_sqrt_fusion
  72.8 0.1 divide_bitcast_fusion
  72.9 0.9 select_reduce_fusion
  73.8 94.8 %all-reduce.6.cloned.1.call-done = f32[1536,1536]{1,0:T(8,128)} async-done(((f32[1536,1536]{1,0:T(8,128)}), f32[1536,1536]{1,0:T(8,128)}) %all-reduce.6.cloned.1.call-update) | async-done | bytes 9437200 | tf_op jit(solution)/shard_map/psum | solution.py:50
  168.6 5.4 %multiply_divide_fusion = f32[1536,1536]{1,0:T(8,128)S(1)} fusion(f32[1536,1536]{1,0:T(8,128)} %all-reduce.6.cloned.1.call-done, f32[1536]{0:T(1024)S(1)} %get-tuple-element.18, f32[1536]{0:T(1024)S(1)} %get-tuple-element.17), kind=kLoop, calls=%fused_computation.4 | loop fusion | flops 11796480 | bytes 18886656 | tf_op jit(solution)/shard_map/div | solution.py:61
  174.0 9.2 %fusion.14 = f32[1536,50]{0,1:T(8,128)S(1)} fusion(f32[1536,1536]{1,0:T(8,128)S(1)} %multiply_divide_fusion, f32[1536,400]{0,1:T(8,128)S(1)} %select_reduce_fusion, s32[]{:T(128)S(6)} %select_n.55, f32[50]{0:T(128)S(1)} %get-tuple-element.16, f32[50]{0:T(128)S(1)} %get-tuple-element.15, f32[50]{0:T(128)S(1)} %get-tuple-element.23, f32[50]{0:T(128)S(1)} %get-tuple-element.24), kind=kOutput, calls=%fused_computation.18 | convolution fusion | flops 1416652800 | bytes 10436608 | tf_op jit(solution)/shard_map/dot_general | solution.py:77
  183.3 10.2 %subtract_bitcast_fusion.1 = f32[1,50,1536]{2,1,0:T(8,128)} fusion(f32[1536,1536]{1,0:T(8,128)S(1)} %multiply_divide_fusion, f32[1536,50]{0,1:T(8,128)S(1)} %fusion.14, f32[1536,400]{0,1:T(8,128)S(1)} %select_reduce_fusion, s32[]{:T(128)S(6)} %select_n.55, f32[50]{0:T(128)S(1)} %get-tuple-element.16, f32[50]{0:T(128)S(1)} %get-tuple-element.15, ...), kind=kOutput, calls=%fused_computation.25 | convolution fusion | flops 1416729600 | bytes 10779652 | tf_op jit(solution)/shard_map/dot_general | solution.py:77
  193.6 0.6 dynamic-slice.4
  194.9 29.4 %all-gather.4.cloned.1.call-done = f32[8,50,1536]{2,1,0:T(8,128)} async-done(((f32[1,50,1536]{2,1,0:T(8,128)}), f32[8,50,1536]{2,1,0:T(8,128)}) %all-gather.4.cloned.1.call-update) | async-done | bytes 2457616 | tf_op jit(solution)/shard_map/all_gather | solution.py:82
  224.3 1.9 reshape.54
  226.2 0.2 divide_convert_fusion
  226.5 1.0 fusion.55
  227.5 9.0 %subtract_bitcast_fusion = f32[2048,400]{0,1:T(8,128)} fusion(bf16[1536,400]{0,1:T(8,128)(2,1)S(1)} %divide_convert_fusion, s32[2048,1536]{1,0:T(8,128)} %param.3, f32[400]{0:T(512)S(1)} %bitcast.32), kind=kOutput, calls=%fused_computation.5 | convolution fusion | flops 2520547328 | bytes 17090112 | tf_op jit(solution)/shard_map/dot_general | solution.py:85
  236.5 65.2 %fusion = f32[2048,104]{0,1:T(8,128)S(1)} fusion(f32[2048,400]{0,1:T(8,128)} %subtract_bitcast_fusion), kind=kCustom, calls=%all-reduce-scatter | all-reduce-scatter fusion | flops 851969 | bytes 4129280
  301.8 1.3 collective-permute-start
  303.1 0.1 select_reduce_fusion.2
  303.2 2.4 collective-permute-done
  305.6 0.5 concatenate
  306.0 0.4 fusion.17
  306.4 11.8 %all-reduce.2 = (f32[100]{0:T(128)S(1)}, f32[100]{0:T(128)S(1)}) all-reduce(f32[100]{0:T(128)S(1)} %get-tuple-element.5, f32[100]{0:T(128)S(1)} %get-tuple-element.4), channel_id=1, replica_groups=mesh['samp'=8,'blk'=4] {'samp'}, use_global_device_ids=true, to_apply=%region_18.19 | all-reduce | flops 200 | bytes 1600 | tf_op jit(solution)/shard_map/psum | solution.py:94
  318.3 10.2 %all-gather.1 = f32[4,100,2]{1,2,0:T(2,128)S(1)} all-gather(f32[1,100,2]{1,2,0:T(2,128)S(1)} %maximum_bitcast_fusion), channel_id=1, replica_groups=mesh['samp'=8,'blk'=4] {'blk'}, dimensions={0}, use_global_device_ids=true | all-gather | bytes 4000 | tf_op jit(solution)/shard_map/all_gather | solution.py:98
  328.5 0.7 reshape.56
  (28 shorter events, 0.3 us)
Async XLA Ops:
  7.2 161.4 %all-reduce.6.cloned.1.call-start = ((), (), s32[]{:S(2)}) async-start(), calls=%async_computation | async-start | bytes 18874368 | tf_op jit(solution)/shard_map/psum | solution.py:50
  26.2 6.4 %copy-start.2 = (s32[2048]{0:T(1024)S(1)}, s32[2048]{0:T(1024)}, u32[]{:S(2)}) copy-start(s32[2048]{0:T(1024)} %param.5) | copy-start | bytes 24580
  26.2 6.5 %copy-start.3 = (f32[2048]{0:T(1024)S(1)}, f32[2048]{0:T(1024)}, u32[]{:S(2)}) copy-start(f32[2048]{0:T(1024)} %param.4) | copy-start | bytes 24580
  26.2 198.1 %all-gather.4.cloned.1.call-start = ((), (), s32[]{:S(2)}) async-start(), calls=%async_computation.1 | async-start | bytes 3096576 | tf_op jit(solution)/shard_map/all_gather | solution.py:82
  26.5 8.3 %copy-start = (s32[2048,1536]{1,0:T(8,128)S(1)}, s32[2048,1536]{1,0:T(8,128)}, u32[]{:S(2)}) copy-start(s32[2048,1536]{1,0:T(8,128)} %param.3) | copy-start | bytes 37748740
  174.0 19.6 %copy-start.4 = (u32[32]{0:T(128)S(1)}, u32[32]{0:T(128)}, u32[]{:S(2)}) copy-start(u32[32]{0:T(128)} %constant.77) | copy-start | bytes 388
  226.2 10.3 %copy-start.1 = (f32[400,1536]{1,0:T(8,128)}, f32[400,1536]{1,0:T(8,128)S(1)}, u32[]{:S(2)}) copy-start(f32[400,1536]{1,0:T(8,128)S(1)} %reshape.54) | copy-start | bytes 7372804
  301.8 3.8 %collective-permute-start = (f32[2048,12]{0,1:T(8,128)S(1)}, f32[2048,12]{0,1:T(8,128)S(1)}, u32[]{:S(2)}, u32[]{:S(2)}) collective-permute-start(f32[2048,12]{0,1:T(8,128)S(1)} %slice), channel_id=1, source_target_pairs={{0,1},{1,2},{2,3},{4,5},{5,6},{6,7},{8,9},{9,10},{10,11},{12,13},{... | collective-permute-start | bytes 294920
Sparse Core Ops, SparseCore 0:
  26.3 142.1 all-reduce.5
  193.6 30.5 all-gather.3
where the time goes:
time: 336 us
  waiting for transfers between devices  127 us (38%)
  blocking collectives  118 us (35%)
  matrix products  54.8 us (16%)
  other arithmetic  15 us (4%)
  between operations  14.9 us (4%)
  local copies, waits for them, and re-layouts  5.64 us (2%)
    psum x1, waiting for transfers between devices, local(): lax.psum((gram_local, local_sum, local_sq, local_geno_pheno, local_pheno_...  94.8 us
    unnamed x1, blocking collectives  65.2 us
    psum x1, blocking collectives, local(): lax.psum((gram_local, local_sum, local_sq, local_geno_pheno, local_pheno_...  30.4 us
    all_gather x1, waiting for transfers between devices, local(): coeff_all = lax.all_gather(coeffs, 'samp', axis=1, tiled=True)  29.4 us
    dot_general x2, matrix products, local(): jnp.dot(ld_block, coeffs, precision=highest)  19.5 us
    dot_general x1, matrix products, local(): jnp.dot(dosage_bf.T, dosage_bf, preferred_element_type=jnp.float32)  19 us
    psum x1, blocking collectives, local(): numerator, denominator = lax.psum((numerator, denominator), 'samp')  11.8 us
    all_gather x1, blocking collectives, local(): fold_scores = lax.all_gather(piece_scores, 'blk', axis=1, tiled=True)  10.2 us
  transfers between devices with their start and end apart: 3, of which 3 were waited for; matrix products, arithmetic and copies ran while one was open for 5% of the time, Pallas kernels for 0%

commit v1 on v0

v1 whole, which is shorter than its diff:
```python
import functools
import math

import jax
import jax.numpy as jnp
from jax import lax
from jax.experimental import pallas as pl
from jax.experimental.pallas import tpu as pltpu
from jax.sharding import PartitionSpec as P

FOLDS = 5
LAMBDAS = 20
SWEEPS = 3
GRID = 400
PER_FOLD = GRID // FOLDS

step_size = 0.6
epsilon = 1e-05
lambda_base = 0.1
lambda_ratio = 1.2
shrink_unit = 0.2
highest = lax.Precision.HIGHEST
MESH = pl.DeviceIdType.MESH


def grid_tables():
    column = jnp.arange(GRID)
    fold_of = column % FOLDS
    levels = column // FOLDS % LAMBDAS
    penalty = lambda_base * jnp.exp(levels.astype(jnp.float32) * math.log(lambda_ratio))
    shrink = shrink_unit * (column // (FOLDS * LAMBDAS) + 1).astype(jnp.float32)
    return (fold_of, penalty, shrink)


def soft_threshold(values, cutoff):
    return values - jnp.clip(values, -cutoff, cutoff)


def flip(index, mask):
    out = index
    for bit in range(mask.bit_length()):
        if mask >> bit & 1:
            out = out + (1 - 2 * (index // (1 << bit) % 2)) * (1 << bit)
    return out


def masks_over(bits):
    out = [0]
    for bit in bits:
        out = out + [m | 1 << bit for m in out]
    return out


def scatter_orders(num):
    bits = num.bit_length() - 1
    return ([0] + list(range(1, bits)), [0] + list(range(bits - 1, 0, -1)))


def scatter_plan(num):
    plan = []
    for order in scatter_orders(num):
        stages = []
        for t in range(len(order)):
            rest = order[t + 1 :]
            got = masks_over(rest)
            got.sort(key=lambda m: tuple(-(m >> b & 1) for b in rest))
            stages.append((order[t], got))
        plan.append(stages)
    return plan


def gather_plan(num):
    plan = []
    for order in scatter_orders(num):
        order = order[::-1]
        plan.append([(bit, masks_over(order[:t])) for t, bit in enumerate(order)])
    return plan


def split3(x):
    hi = x.astype(jnp.bfloat16)
    rest = x - hi.astype(jnp.float32)
    mid = rest.astype(jnp.bfloat16)
    low = (rest - mid.astype(jnp.float32)).astype(jnp.bfloat16)
    return hi, mid, low


def kernel(
    num,
    nblk,
    sample_count,
    snp_total,
    gram,
    dosage,
    pheno_row,
    fold_row,
    pheno_parts,
    fold_parts,
    table,
    perm,
    coeff_out,
    score_out,
    rs_buf,
    stat_buf,
    col_ref,
    target_ref,
    c1_ref,
    c2_ref,
    ld_ref,
    wt_ref,
    sel_buf,
    sel_recv,
    fin_samp,
    fin_blk,
    rs_send,
    rs_recv,
    stat_send,
    stat_recv,
    ag_send,
    ag_recv,
    sel_send,
    sel_rsem,
    fin_send,
    fin_rsem,
    fbl_send,
    fbl_rsem,
):
    me = lax.axis_index("samp")
    zz = lax.axis_index("blk")
    width = gram.shape[0]
    rows = width // num
    half = width // 2

    barrier = pltpu.get_barrier_semaphore()
    for e in range(1, num):
        pl.semaphore_signal(barrier, inc=1, device_id={"samp": flip(me, e)}, device_id_type=MESH)
    for k in range(1, nblk):
        pl.semaphore_signal(
            barrier, inc=1, device_id={"blk": lax.rem(zz + k, nblk)}, device_id_type=MESH
        )
    pl.semaphore_wait(barrier, num - 1 + nblk - 1)

    plan = scatter_plan(num)
    slot_of = {}
    for h in range(2):
        for t, (_, got) in enumerate(plan[h]):
            for e in got:
                slot_of[h, t, e] = len(slot_of)

    def gram_block(e, h):
        return gram.at[pl.ds(pl.multiple_of(flip(me, e) * rows, rows), rows), pl.ds(h * half, half)]

    def rs_copy(h, t, got):
        bit = plan[h][t][0]
        sent = got | 1 << bit
        src = gram_block(sent, h) if t == 0 else rs_buf.at[slot_of[h, t - 1, sent]]
        slot = slot_of[h, t, got]
        return pltpu.make_async_remote_copy(
            src_ref=src,
            dst_ref=rs_buf.at[slot],
            send_sem=rs_send.at[slot],
            recv_sem=rs_recv.at[slot],
            device_id={"samp": flip(me, 1 << bit)},
            device_id_type=MESH,
        )

    stages = len(plan[0])
    for pos in range(len(plan[0][0][1])):
        for h in range(2):
            rs_copy(h, 0, plan[h][0][1][pos]).start()

    pheno = pheno_row[...]
    fold = fold_row[...]
    pieces = [jnp.ones(pheno.shape, jnp.bfloat16).astype(jnp.float32)]
    masked = [jnp.where(fold == k, pheno, 0.0) for k in range(FOLDS)]
    parts = [split3(x) for x in masked]
    for which in range(3):
        for k in range(FOLDS):
            pieces.append(parts[k][which].astype(jnp.float32))
    left = jnp.concatenate(pieces, axis=0).astype(jnp.bfloat16)
    geno = dosage[...]
    prod = jnp.dot(left, geno, preferred_element_type=jnp.float32)
    squares = jnp.dot(
        jnp.ones((16, geno.shape[0]), jnp.bfloat16), geno * geno, preferred_element_type=jnp.float32
    )
    lane = lax.broadcasted_iota(jnp.int32, (1, width), 1)
    extra = jnp.zeros((1, width), jnp.float32)
    for k in range(FOLDS):
        extra = jnp.where(lane == k, jnp.sum(masked[k], axis=1, keepdims=True), extra)
        count = jnp.sum(jnp.where(fold == k, 1.0, 0.0), axis=1, keepdims=True)
        extra = jnp.where(lane == 8 + k, count, extra)
    stat_buf[me] = jnp.concatenate(
        [
            prod[0:1],
            squares[0:1],
            (prod[1 + 2 * FOLDS : 1 + 3 * FOLDS] + prod[1 + FOLDS : 1 + 2 * FOLDS])
            + prod[1 : 1 + FOLDS],
            extra,
        ],
        axis=0,
    )

    def to_samp(buf, e, send, recv, holder):
        return pltpu.make_async_remote_copy(
            src_ref=buf.at[holder],
            dst_ref=buf.at[holder],
            send_sem=send.at[e - 1],
            recv_sem=recv.at[e - 1],
            device_id={"samp": flip(me, e)},
            device_id_type=MESH,
        )

    for e in range(1, num):
        to_samp(stat_buf, e, stat_send, stat_recv, me).start()

    def rs_stage(t):
        for pos in range(len(plan[0][t][1])):
            for h in range(2):
                got = plan[h][t][1][pos]
                slot = slot_of[h, t, got]
                rs_copy(h, t, got).wait_recv()
                prev = gram_block(got, h) if t == 0 else rs_buf.at[slot_of[h, t - 1, got]]
                rs_buf[slot] = rs_buf[slot] + prev[...]
                if t + 1 < stages and got >> plan[h][t + 1][0] & 1:
                    rs_copy(h, t + 1, got & ~(1 << plan[h][t + 1][0])).start()

    rs_stage(0)

    for e in range(1, num):
        to_samp(stat_buf, e, stat_send, stat_recv, flip(me, e)).wait_recv()
    total = stat_buf[0]
    for d in range(1, num):
        total = total + stat_buf[d]
    mean_row = total[0:1] / sample_count
    scale_row = jnp.sqrt(total[1:2] / sample_count - mean_row * mean_row + epsilon)
    turned = total.T
    mean_col = turned[:, 0:1] / sample_count
    scale_col = jnp.sqrt(turned[:, 1:2] / sample_count - mean_col * mean_col + epsilon)
    col_ref[:, 0:1] = mean_col
    col_ref[:, 1:2] = scale_col
    fold_pheno = [total[7:8, k : k + 1] for k in range(FOLDS)]
    counts = [total[7:8, 8 + k : 9 + k] for k in range(FOLDS)]
    pheno_all = sum(fold_pheno[1:], fold_pheno[0])
    geno_pheno = [turned[:, 2 + k : 3 + k] for k in range(FOLDS)]
    geno_pheno_all = sum(geno_pheno[1:], geno_pheno[0])
    thresh = table[0:1, :]
    shrink = table[1:2, :]
    fold_of = table[2:3, :]
    target = jnp.zeros((width, GRID), jnp.float32)
    for k in range(FOLDS):
        z = (geno_pheno_all - geno_pheno[k] - (pheno_all - fold_pheno[k]) * mean_col) / (
            scale_col * jnp.sqrt(sample_count - counts[k])
        )
        target = jnp.where(fold_of == float(k), z, target)
    target_ref[...] = target
    c1_ref[...] = soft_threshold(step_size * target, thresh)

    for t in range(1, stages):
        rs_stage(t)

    mine = pl.ds(pl.multiple_of(me * rows, rows), rows)
    mean_mine = col_ref[mine, 0:1]
    scale_mine = col_ref[mine, 1:2]
    for h in range(2):
        cols = slice(h * half, (h + 1) * half)
        summed = rs_buf[slot_of[h, stages - 1, 0]]
        ld_ref[:, cols] = (summed / sample_count - mean_mine * mean_row[:, cols]) / (
            scale_mine * scale_row[:, cols]
        )

    def sweep(full, out):
        held = full[mine, :]
        gradient = (
            (1.0 - shrink)
            * jnp.dot(ld_ref[...], full[...], precision=highest, preferred_element_type=jnp.float32)
            + shrink * held
            - target_ref[mine, :]
        )
        out[mine, :] = soft_threshold(held - step_size * gradient, thresh)

    aplan = gather_plan(num)
    aslot = {}
    for h in range(2):
        for t, (_, held) in enumerate(aplan[h]):
            for e in held:
                aslot[h, t, e] = len(aslot)
    part = rows // 2

    def ag_copy(buf, which, h, t, e, owner):
        place = buf.at[pl.ds(pl.multiple_of(owner * rows + h * part, part), part), :]
        slot = aslot[h, t, e]
        return pltpu.make_async_remote_copy(
            src_ref=place,
            dst_ref=place,
            send_sem=ag_send.at[which, slot],
            recv_sem=ag_recv.at[which, slot],
            device_id={"samp": flip(me, 1 << aplan[h][t][0])},
            device_id_type=MESH,
        )

    def gather(buf, which):
        def arrived(h, first, e):
            for t in range(first, len(aplan[h])):
                ag_copy(buf, which, h, t, e, flip(me, e)).start()

        for h in range(2):
            arrived(h, 0, 0)
        for t in range(len(aplan[0])):
            for pos in range(len(aplan[0][t][1])):
                for h in range(2):
                    bit, held = aplan[h][t]
                    e = held[pos]
                    got = e | 1 << bit
                    ag_copy(buf, which, h, t, e, flip(me, got)).wait_recv()
                    arrived(h, t + 1, got)

    def gather_end(buf, which):
        for h in range(2):
            for t, (_, held) in enumerate(aplan[h]):
                for e in held:
                    ag_copy(buf, which, h, t, e, flip(me, e)).wait_send()

    sweep(c1_ref, c2_ref)
    gather(c2_ref, 0)
    sweep(c2_ref, coeff_out)
    gather(coeff_out, 1)

    weighted = (coeff_out[...] / col_ref[:, 1:2]).astype(jnp.bfloat16)
    turned_w = lax.dot_general(
        perm[...], weighted, (((1,), (1,)), ((), ())), preferred_element_type=jnp.float32
    )
    wt_ref[...] = turned_w.astype(jnp.bfloat16)
    offset = jnp.sum(turned_w * mean_row, axis=1, keepdims=True)

    people = fold_parts.shape[2]

    def sel_copy(k):
        return pltpu.make_async_remote_copy(
            src_ref=sel_buf.at[k],
            dst_ref=sel_recv.at[k - 1],
            send_sem=sel_send.at[k - 1],
            recv_sem=sel_rsem.at[k - 1],
            device_id={"blk": lax.rem(zz + k, nblk)},
            device_id_type=MESH,
        )

    for k in list(range(1, nblk)) + [0]:
        peer = lax.rem(zz + k, nblk)
        some = dosage[pl.ds(pl.multiple_of(peer * people, people), people), :]
        value = (
            lax.dot_general(
                wt_ref[...], some, (((1,), (1,)), ((), ())), preferred_element_type=jnp.float32
            )
            - offset
        )
        ids = fold_parts[peer]
        chosen = jnp.zeros((PER_FOLD, people), jnp.float32)
        for f in range(FOLDS):
            chosen = jnp.where(ids == f, value[f * PER_FOLD : (f + 1) * PER_FOLD], chosen)
        sel_buf[k] = chosen
        if k:
            sel_copy(k).start()
    predicted = sel_buf[0]
    for k in range(1, nblk):
        sel_copy(k).wait_recv()
        predicted = predicted + sel_recv[k - 1]
    predicted = predicted / math.sqrt(snp_total)
    ids = fold_parts[zz]
    in_fold = lax.broadcasted_iota(jnp.int32, (8, people), 0) == ids
    lanes = (((1,), (1,)), ((), ()))
    numer = lax.dot_general(
        jnp.where(in_fold, pheno_parts[zz], 0.0),
        predicted,
        lanes,
        precision=highest,
        preferred_element_type=jnp.float32,
    )
    denom = lax.dot_general(
        jnp.where(in_fold, 1.0, 0.0),
        predicted * predicted,
        lanes,
        precision=highest,
        preferred_element_type=jnp.float32,
    )
    both = jnp.concatenate([numer, denom], axis=0)
    fin_samp[me] = jnp.concatenate(
        [both, jnp.zeros((16, fin_samp.shape[2] - PER_FOLD), jnp.float32)], axis=1
    )
    for e in range(1, num):
        to_samp(fin_samp, e, fin_send, fin_rsem, me).start()
    for e in range(1, num):
        to_samp(fin_samp, e, fin_send, fin_rsem, flip(me, e)).wait_recv()
    both = fin_samp[0]
    for d in range(1, num):
        both = both + fin_samp[d]
    fin_blk[zz] = both

    def fbl_copy(k, holder):
        return pltpu.make_async_remote_copy(
            src_ref=fin_blk.at[holder],
            dst_ref=fin_blk.at[holder],
            send_sem=fbl_send.at[k - 1],
            recv_sem=fbl_rsem.at[k - 1],
            device_id={"blk": lax.rem(zz + k, nblk)},
            device_id_type=MESH,
        )

    for k in range(1, nblk):
        fbl_copy(k, zz).start()
    for k in range(1, nblk):
        fbl_copy(k, lax.rem(zz + nblk - k, nblk)).wait_recv()
    both = fin_blk[0]
    for d in range(1, nblk):
        both = both + fin_blk[d]
    row = lax.broadcasted_iota(jnp.int32, (16, 1), 0)
    count_col = jnp.ones((16, 1), jnp.float32)
    for k in range(FOLDS):
        count_col = jnp.where((row == k) | (row == 8 + k), counts[k], count_col)
    score_out[...] = both / count_col

    for h in range(2):
        for t in range(stages):
            for got in plan[h][t][1]:
                rs_copy(h, t, got).wait_send()
    for e in range(1, num):
        to_samp(stat_buf, e, stat_send, stat_recv, me).wait_send()
        to_samp(fin_samp, e, fin_send, fin_rsem, me).wait_send()
    gather_end(c2_ref, 0)
    gather_end(coeff_out, 1)
    for k in range(1, nblk):
        sel_copy(k).wait_send()
        fbl_copy(k, zz).wait_send()


def local(genotypes, phenotype, fold_ids):
    num_rows, width = genotypes.shape
    num = lax.axis_size("samp")
    nblk = lax.axis_size("blk")
    people = num_rows // nblk
    rows = width // num
    dosage = genotypes.astype(jnp.bfloat16)
    gram = jnp.dot(dosage.T, dosage, preferred_element_type=jnp.float32)
    fold_of, penalty, shrink = grid_tables()
    table = jnp.concatenate(
        [
            jnp.stack([step_size * penalty, shrink, fold_of.astype(jnp.float32)]),
            jnp.zeros((5, GRID), jnp.float32),
        ]
    )
    order = jnp.arange(GRID)
    perm = (
        (order % PER_FOLD * FOLDS + order // PER_FOLD)[:, None] == order[None, :]
    ).astype(jnp.bfloat16)
    rs_slots = 2 * (num - 1)
    ag_slots = 2 * (num - 1)
    dma = pltpu.SemaphoreType.DMA
    f32 = jnp.float32
    coeff_all, scores = pl.pallas_call(
        functools.partial(kernel, num, nblk, num_rows * num, width * nblk),
        out_shape=(
            jax.ShapeDtypeStruct((width, GRID), f32),
            jax.ShapeDtypeStruct((16, 128), f32),
        ),
        in_specs=[pl.BlockSpec(memory_space=pltpu.VMEM)] * 8,
        out_specs=(pl.BlockSpec(memory_space=pltpu.VMEM),) * 2,
        scratch_shapes=[
            pltpu.VMEM((rs_slots, rows, width // 2), f32),
            pltpu.VMEM((num, 8, width), f32),
            pltpu.VMEM((width, 8), f32),
            pltpu.VMEM((width, GRID), f32),
            pltpu.VMEM((width, GRID), f32),
            pltpu.VMEM((width, GRID), f32),
            pltpu.VMEM((rows, width), f32),
            pltpu.VMEM((GRID, width), jnp.bfloat16),
            pltpu.VMEM((nblk, PER_FOLD, people), f32),
            pltpu.VMEM((nblk - 1, PER_FOLD, people), f32),
            pltpu.VMEM((num, 16, 128), f32),
            pltpu.VMEM((nblk, 16, 128), f32),
            dma((rs_slots,)),
            dma((rs_slots,)),
            dma((num - 1,)),
            dma((num - 1,)),
            dma((2, ag_slots)),
            dma((2, ag_slots)),
            dma((nblk - 1,)),
            dma((nblk - 1,)),
            dma((num - 1,)),
            dma((num - 1,)),
            dma((nblk - 1,)),
            dma((nblk - 1,)),
        ],
        compiler_params=pltpu.CompilerParams(
            collective_id=0, has_side_effects=True, vmem_limit_bytes=62 * 1024 * 1024
        ),
    )(
        gram,
        dosage,
        phenotype.reshape(1, num_rows),
        fold_ids.reshape(1, num_rows),
        phenotype.reshape(nblk, 1, people),
        fold_ids.reshape(nblk, 1, people),
        table,
        perm,
    )
    scores = scores.reshape(2, 8, 128)[:, :FOLDS, :PER_FOLD]
    return (coeff_all, scores.transpose(0, 2, 1).reshape(2, GRID))


def solution(mesh):
    return jax.shard_map(
        local,
        mesh=mesh,
        in_specs=(P("samp", "blk"), P("samp"), P("samp")),
        out_specs=(P("blk", None), P()),
        check_vma=False,
    )
```

time: 336 us -> 151 us (0.45)
  waiting for transfers between devices: 127 us -> 0 us
  Pallas kernels: 0 us -> 122 us
  blocking collectives: 118 us -> 0 us
  matrix products: 54.8 us -> 12.6 us
  between operations: 14.9 us -> 0.68 us
  other arithmetic: 15 us -> 7.87 us
    pallas_call x0 -> x1, Pallas kernels: none -> 122 us  [local(): pl.pallas_call(functools.partial(kernel, num, nblk, num_rows * num, width...]
    psum x1 -> x0, waiting for transfers between devices: 94.8 us -> none  [local(): lax.psum((gram_local, local_sum, local_sq, local_geno_pheno, local_pheno_...]
    unnamed x1 -> x0, blocking collectives: 65.2 us -> none
    psum x2 -> x0, blocking collectives: 42.2 us -> none  [the longest x1 30.4 us: local(): lax.psum((gram_local, local_sum, local_sq, local_geno_pheno, local_pheno_...]
    dot_general x6 -> x1, matrix products: 54.8 us -> 12.6 us  [local(): gram = jnp.dot(dosage.T, dosage, preferred_element_type=jnp.float32)]
    all_gather x1 -> x0, waiting for transfers between devices: 29.4 us -> none  [local(): coeff_all = lax.all_gather(coeffs, 'samp', axis=1, tiled=True)]
    all_gather x1 -> x0, blocking collectives: 10.2 us -> none  [local(): fold_scores = lax.all_gather(piece_scores, 'blk', axis=1, tiled=True)]
    reduce_sum x8 -> x0, other arithmetic: 8.36 us -> none  [the longest x1 6.06 us: local(): local_sum = jnp.sum(genotypes, axis=0).astype(jnp.float32)]
  transfers between devices with their start and end apart: 3 -> 0, of which waited for: 3 -> 0; matrix products, arithmetic and copies ran while one was open for 5% -> 0% of each run, Pallas kernels for 0% -> 0%
where the time goes in v1:
time: 151 us
  Pallas kernels  122 us (81%)
  matrix products  12.6 us (8%)
  other arithmetic  7.87 us (5%)
  local copies, waits for them, and re-layouts  7.68 us (5%)
    pallas_call x1, Pallas kernels, local(): pl.pallas_call(functools.partial(kernel, num, nblk, num_rows * num, width...  122 us
    dot_general x1, matrix products, local(): gram = jnp.dot(dosage.T, dosage, preferred_element_type=jnp.float32)  12.6 us
    unnamed x4, local copies, waits for them, and re-layouts  6.85 us
    convert_element_type x1, other arithmetic, local(): dosage = genotypes.astype(jnp.bfloat16)  6.25 us

profile of v1, /device:TPU:0, one launch (start us, length us, event | category | flops | bytes accessed | tf_op | source)
XLA Modules:
  0.0 151.2 jit_solution(15101531859492053218)
XLA Ops:
  0.6 0.1 pad.3.clone
  0.8 0.7 maximum_maximum_fusion.table
  1.5 0.9 fusion.perm
  2.3 6.3 %convert_element_type.36.dosage = bf16[2048,1536]{1,0:T(8,128)(2,1)S(1)} convert(s32[2048,1536]{1,0:T(8,128)} %param.3) | non-fusion elementwise | flops 3145728 | bytes 18874368 | tf_op jit(solution)/shard_map/convert_element_type | solution.py:441
  8.6 0.0 copy-start
  8.6 2.7 %copy-done = bf16[2048,1536]{1,0:T(8,128)(2,1)} copy-done((bf16[2048,1536]{1,0:T(8,128)(2,1)}, bf16[2048,1536]{1,0:T(8,128)(2,1)S(1)}, u32[]{:S(2)}) %copy-start) | copy-done | bytes 6291480
  11.3 12.6 %fusion.16.gram = f32[1536,1536]{1,0:T(8,128)} fusion(bf16[2048,1536]{1,0:T(8,128)(2,1)S(1)} %convert_element_type.36.dosage), kind=kOutput, calls=%fused_computation.32 | convolution fusion | flops 9663676416 | bytes 15728640 | tf_op jit(solution)/shard_map/dot_general | solution.py:442
  23.9 122.4 %shard_map.50 = (f32[1536,400]{1,0:T(8,128)}, f32[16,128]{1,0:T(8,128)}) custom-call(f32[1536,1536]{1,0:T(8,128)} %fusion.16.gram, bf16[2048,1536]{1,0:T(8,128)(2,1)} %copy-done, f32[1,2048]{1,0:T(1,128)} %bitcast.10, s32[1,2048]{1,0:T(1,128)} %bitcast.12, f32[4,1,512]{2,1,0:T(1,128)} %bitcast.11, s32[4,1,512]{2,1,0:T(1,128)} %bitcast.13, ...), custom_call_target="tpu_custom_call" | custom-call | tf_op jit(solution)/shard_map/pallas_call | solution.py:458
  146.3 3.4 %copy.8 = f32[1536,400]{0,1:T(8,128)} copy(f32[1536,400]{1,0:T(8,128)} %get-tuple-element.8) | data formatting | bytes 4915200
  149.7 0.8 copy.9
  150.5 0.8 reshape.162
  (4 shorter events, 0.1 us)
Async XLA Ops:
  8.6 2.7 %copy-start = (bf16[2048,1536]{1,0:T(8,128)(2,1)}, bf16[2048,1536]{1,0:T(8,128)(2,1)S(1)}, u32[]{:S(2)}) copy-start(bf16[2048,1536]{1,0:T(8,128)(2,1)S(1)} %convert_element_type.36.dosage) | copy-start | bytes 18874372

commit v2 on v1

--- a/solution.py
+++ b/solution.py
@@ -3,6 +3,7 @@
 
 import jax
 import jax.numpy as jnp
+import numpy as np
 from jax import lax
 from jax.experimental import pallas as pl
 from jax.experimental.pallas import tpu as pltpu
@@ -24,11 +25,11 @@
 
 
 def grid_tables():
-    column = jnp.arange(GRID)
+    column = np.arange(GRID)
     fold_of = column % FOLDS
     levels = column // FOLDS % LAMBDAS
-    penalty = lambda_base * jnp.exp(levels.astype(jnp.float32) * math.log(lambda_ratio))
-    shrink = shrink_unit * (column // (FOLDS * LAMBDAS) + 1).astype(jnp.float32)
+    penalty = lambda_base * np.exp(levels * math.log(lambda_ratio))
+    shrink = shrink_unit * (column // (FOLDS * LAMBDAS) + 1)
     return (fold_of, penalty, shrink)
 
 
@@ -90,8 +91,7 @@
     nblk,
     sample_count,
     snp_total,
-    gram,
-    dosage,
+    genotypes,
     pheno_row,
     fold_row,
     pheno_parts,
@@ -100,18 +100,23 @@
     perm,
     coeff_out,
     score_out,
+    raw,
+    dosage,
+    gram,
     rs_buf,
     stat_buf,
     col_ref,
     target_ref,
     c1_ref,
     c2_ref,
-    ld_ref,
+    ld_hi,
+    ld_lo,
     wt_ref,
     sel_buf,
     sel_recv,
     fin_samp,
     fin_blk,
+    load_sem,
     rs_send,
     rs_recv,
     stat_send,
@@ -127,9 +132,18 @@
 ):
     me = lax.axis_index("samp")
     zz = lax.axis_index("blk")
-    width = gram.shape[0]
+    num_rows, width = genotypes.shape
     rows = width // num
     half = width // 2
+    loads = load_sem.shape[0]
+    step = num_rows // loads
+
+    def load(i):
+        piece = pl.ds(i * step, step)
+        return pltpu.make_async_copy(genotypes.at[piece, :], raw.at[piece, :], load_sem.at[i])
+
+    for i in range(loads):
+        load(i).start()
 
     barrier = pltpu.get_barrier_semaphore()
     for e in range(1, num):
@@ -148,7 +162,7 @@
                 slot_of[h, t, e] = len(slot_of)
 
     def gram_block(e, h):
-        return gram.at[pl.ds(pl.multiple_of(flip(me, e) * rows, rows), rows), pl.ds(h * half, half)]
+        return gram.at[flip(me, e), :, pl.ds(h * half, half)]
 
     def rs_copy(h, t, got):
         bit = plan[h][t][0]
@@ -165,9 +179,47 @@
         )
 
     stages = len(plan[0])
-    for pos in range(len(plan[0][0][1])):
+    for i in range(loads):
+        load(i).wait()
+        dosage[i * step : (i + 1) * step, :] = raw[i * step : (i + 1) * step, :].astype(jnp.bfloat16)
+
+    def rs_take(t, gots):
+        for pos in range(len(gots[0])):
+            for h in range(2):
+                got = gots[h][pos]
+                slot = slot_of[h, t, got]
+                rs_copy(h, t, got).wait_recv()
+                prev = gram_block(got, h) if t == 0 else rs_buf.at[slot_of[h, t - 1, got]]
+                rs_buf[slot] = rs_buf[slot] + prev[...]
+                if t + 1 < stages and got >> plan[h][t + 1][0] & 1:
+                    rs_copy(h, t + 1, got & ~(1 << plan[h][t + 1][0])).start()
+
+    unit = 1
+    while unit * rows % 128 and unit * 2 <= num:
+        unit *= 2
+
+    def gram_unit(m):
+        first = flip(me, m) // unit
+        span = pl.ds(pl.multiple_of(first * (unit * rows), unit * rows), unit * rows)
+        left = dosage[:, span].T
         for h in range(2):
-            rs_copy(h, 0, plan[h][0][1][pos]).start()
+            out = jnp.dot(
+                left,
+                dosage[:, h * half : (h + 1) * half],
+                preferred_element_type=jnp.float32,
+            )
+            for j in range(unit):
+                gram[first * unit + j, :, h * half : (h + 1) * half] = out[j * rows : (j + 1) * rows]
+        for h in range(2):
+            for got in plan[h][0][1]:
+                if got // unit * unit == m:
+                    rs_copy(h, 0, got).start()
+
+    def unit_take(m):
+        rs_take(0, [[got for got in plan[h][0][1] if got // unit * unit == m] for h in range(2)])
+
+    units = [m for m in plan[0][0][1] if m % unit == 0]
+    gram_unit(units[0])
 
     pheno = pheno_row[...]
     fold = fold_row[...]
@@ -213,18 +265,10 @@
     for e in range(1, num):
         to_samp(stat_buf, e, stat_send, stat_recv, me).start()
 
-    def rs_stage(t):
-        for pos in range(len(plan[0][t][1])):
-            for h in range(2):
-                got = plan[h][t][1][pos]
-                slot = slot_of[h, t, got]
-                rs_copy(h, t, got).wait_recv()
-                prev = gram_block(got, h) if t == 0 else rs_buf.at[slot_of[h, t - 1, got]]
-                rs_buf[slot] = rs_buf[slot] + prev[...]
-                if t + 1 < stages and got >> plan[h][t + 1][0] & 1:
-                    rs_copy(h, t + 1, got & ~(1 << plan[h][t + 1][0])).start()
-
-    rs_stage(0)
+    for i in range(1, len(units)):
+        gram_unit(units[i])
+        unit_take(units[i - 1])
+    unit_take(units[-1])
 
     for e in range(1, num):
         to_samp(stat_buf, e, stat_send, stat_recv, flip(me, e)).wait_recv()
@@ -256,7 +300,7 @@
     c1_ref[...] = soft_threshold(step_size * target, thresh)
 
     for t in range(1, stages):
-        rs_stage(t)
+        rs_take(t, [plan[h][t][1] for h in range(2)])
 
     mine = pl.ds(pl.multiple_of(me * rows, rows), rows)
     mean_mine = col_ref[mine, 0:1]
@@ -264,15 +308,24 @@
     for h in range(2):
         cols = slice(h * half, (h + 1) * half)
         summed = rs_buf[slot_of[h, stages - 1, 0]]
-        ld_ref[:, cols] = (summed / sample_count - mean_mine * mean_row[:, cols]) / (
+        block = (summed / sample_count - mean_mine * mean_row[:, cols]) / (
             scale_mine * scale_row[:, cols]
         )
+        upper = block.astype(jnp.bfloat16)
+        ld_hi[:, cols] = upper
+        ld_lo[:, cols] = (block - upper.astype(jnp.float32)).astype(jnp.bfloat16)
 
     def sweep(full, out):
         held = full[mine, :]
+        whole = full[...]
+        upper = whole.astype(jnp.bfloat16)
+        lower = (whole - upper.astype(jnp.float32)).astype(jnp.bfloat16)
+        applied = (
+            jnp.dot(ld_hi[...], lower, preferred_element_type=jnp.float32)
+            + jnp.dot(ld_lo[...], upper, preferred_element_type=jnp.float32)
+        ) + jnp.dot(ld_hi[...], upper, preferred_element_type=jnp.float32)
         gradient = (
-            (1.0 - shrink)
-            * jnp.dot(ld_ref[...], full[...], precision=highest, preferred_element_type=jnp.float32)
+            (1.0 - shrink) * applied
             + shrink * held
             - target_ref[mine, :]
         )
@@ -438,19 +491,17 @@
     nblk = lax.axis_size("blk")
     people = num_rows // nblk
     rows = width // num
-    dosage = genotypes.astype(jnp.bfloat16)
-    gram = jnp.dot(dosage.T, dosage, preferred_element_type=jnp.float32)
     fold_of, penalty, shrink = grid_tables()
-    table = jnp.concatenate(
-        [
-            jnp.stack([step_size * penalty, shrink, fold_of.astype(jnp.float32)]),
-            jnp.zeros((5, GRID), jnp.float32),
-        ]
-    )
-    order = jnp.arange(GRID)
-    perm = (
-        (order % PER_FOLD * FOLDS + order // PER_FOLD)[:, None] == order[None, :]
-    ).astype(jnp.bfloat16)
+    zero = np.zeros(GRID)
+    table = jnp.asarray(
+        np.stack([step_size * penalty, shrink, fold_of] + [zero] * 5).astype(np.float32)
+    )
+    order = np.arange(GRID)
+    perm = jnp.asarray(
+        ((order % PER_FOLD * FOLDS + order // PER_FOLD)[:, None] == order[None, :]).astype(
+            jnp.bfloat16
+        )
+    )
     rs_slots = 2 * (num - 1)
     ag_slots = 2 * (num - 1)
     dma = pltpu.SemaphoreType.DMA
@@ -461,21 +512,27 @@
             jax.ShapeDtypeStruct((width, GRID), f32),
             jax.ShapeDtypeStruct((16, 128), f32),
         ),
-        in_specs=[pl.BlockSpec(memory_space=pltpu.VMEM)] * 8,
+        in_specs=[pl.BlockSpec(memory_space=pl.ANY)]
+        + [pl.BlockSpec(memory_space=pltpu.VMEM)] * 6,
         out_specs=(pl.BlockSpec(memory_space=pltpu.VMEM),) * 2,
         scratch_shapes=[
+            pltpu.VMEM((num_rows, width), jnp.int32),
+            pltpu.VMEM((num_rows, width), jnp.bfloat16),
+            pltpu.VMEM((num, rows, width), f32),
             pltpu.VMEM((rs_slots, rows, width // 2), f32),
             pltpu.VMEM((num, 8, width), f32),
             pltpu.VMEM((width, 8), f32),
             pltpu.VMEM((width, GRID), f32),
             pltpu.VMEM((width, GRID), f32),
             pltpu.VMEM((width, GRID), f32),
-            pltpu.VMEM((rows, width), f32),
+            pltpu.VMEM((rows, width), jnp.bfloat16),
+            pltpu.VMEM((rows, width), jnp.bfloat16),
             pltpu.VMEM((GRID, width), jnp.bfloat16),
             pltpu.VMEM((nblk, PER_FOLD, people), f32),
             pltpu.VMEM((nblk - 1, PER_FOLD, people), f32),
             pltpu.VMEM((num, 16, 128), f32),
             pltpu.VMEM((nblk, 16, 128), f32),
+            dma((8,)),
             dma((rs_slots,)),
             dma((rs_slots,)),
             dma((num - 1,)),
@@ -493,8 +550,7 @@
             collective_id=0, has_side_effects=True, vmem_limit_bytes=62 * 1024 * 1024
         ),
     )(
-        gram,
-        dosage,
+        genotypes,
         phenotype.reshape(1, num_rows),
         fold_ids.reshape(1, num_rows),
         phenotype.reshape(nblk, 1, people),

time: 151 us -> 126 us (0.83)
  matrix products: 12.6 us -> 0 us
  other arithmetic: 7.87 us -> 0 us
  local copies, waits for them, and re-layouts: 7.68 us -> 4.23 us
    dot_general x1 -> x0, matrix products: 12.6 us -> none  [local(): gram = jnp.dot(dosage.T, dosage, preferred_element_type=jnp.float32)]
    convert_element_type x3 -> x0, other arithmetic: 7.15 us -> none  [the longest x1 6.25 us: local(): dosage = genotypes.astype(jnp.bfloat16)]
    unnamed x4, local copies, waits for them, and re-layouts: 6.85 us -> 3.47 us
where the time goes in v2:
time: 126 us
  Pallas kernels  121 us (96%)
  local copies, waits for them, and re-layouts  4.23 us (3%)
    pallas_call x1, Pallas kernels, local(): pl.pallas_call(functools.partial(kernel, num, nblk, num_rows * num, width...  121 us
    unnamed x4, local copies, waits for them, and re-layouts  3.47 us

profile of v2, /device:TPU:0, one launch (start us, length us, event | category | flops | bytes accessed | tf_op | source)
XLA Modules:
  0.0 126.0 jit_solution(13416802301688059669)
XLA Ops:
  0.6 121.1 %shard_map.68 = (f32[1536,400]{1,0:T(8,128)}, f32[16,128]{1,0:T(8,128)}) custom-call(s32[2048,1536]{1,0:T(8,128)} %genotypes.1, f32[1,2048]{1,0:T(1,128)} %bitcast.8, s32[1,2048]{1,0:T(1,128)} %bitcast.10, f32[4,1,512]{2,1,0:T(1,128)} %bitcast.9, s32[4,1,512]{2,1,0:T(1,128)} %bitcast.11, f32[8,400]{1,0:T(8,128)} %constant.4.clone.table, ...), custom_call_target="tpu_custom_call" | custom-call | tf_op jit(solution)/shard_map/pallas_call | solution.py:509
  121.7 0.0 copy-start
  121.7 3.4 %copy.10 = f32[1536,400]{0,1:T(8,128)} copy(f32[1536,400]{1,0:T(8,128)} %get-tuple-element.8) | data formatting | bytes 4915200
  125.1 0.0 copy-done
  125.1 0.1 copy.11
  125.2 0.8 reshape.27
Async XLA Ops:
  121.7 3.4 %copy-start = (f32[16,128]{1,0:T(8,128)S(1)}, f32[16,128]{1,0:T(8,128)}, u32[]{:S(2)}) copy-start(f32[16,128]{1,0:T(8,128)} %get-tuple-element.5) | copy-start | bytes 24580
